TPU v7x, 512 devices: a whole 4x4x16 slice. The times are simulated.
512 devices in a mesh: group: 16 (over z), sub: 32 (over x, y, core).
Axes of the slice: x: 4, y: 4, z: 16, core: 2. Of those that a mesh axis runs over, the one named last changes fastest.
Arguments:
- couplings: float32 [512, 6, 384, 384], P(('group', 'sub')), may hold values from -0.3125 to 0.3125
- mode_rows: float32 [786432, 128], P(('group', 'sub')), may hold values from -1.5 to 1.5
- coarse_basis: float32 [65536, 256], P(('group', 'sub')), may hold values from -0.09375 to 0.09375
- stiffness: float32 [512, 1536], P(('group', 'sub')), may hold values from 0.005 to 0.05
- own_face: int32 [512, 6], P(('group', 'sub')), may hold values from 0 to 3, as said below
- neighbour_face: int32 [512, 6], P(('group', 'sub')), may hold values from 0 to 3, as said below
- present: int32 [512, 6], P(('group', 'sub')), may hold values from 0 to 1, as said below
Outputs:
- coarse_blocks: float32 [512, 7, 128, 128], P(('group', 'sub'))
- coarse_group: float32 [16, 3, 256, 256], P('group', None, 'sub')
Inputs may be any that keep to these rules, and one draw needn't show every extreme that they name: `own_face`: face block index of the subdomain's own unknowns toward each direction. Wherever present is 1, neighbour_face[d, k] equals own_face of the neighbour n(d, k) at the opposite direction (0 and 1, 2 and 3, 4 and 5 are opposite). `present`: 0 wherever the neighbour lies outside the group's plane of 4 columns and 8 rows or outside the groups, and on broken couplings; a coupling is intact on both sides or on neither.
All inputs are finite; a program needn't handle non-finite values.
Results may differ from a plain program's by a relative error of at most 0.0003.
Values sent between devices are 32-bit elements; how exact they have to be, the bound alone decides.
No kernel may reach another device: no remote copies, remote signals or barrier semaphores. Data moves between devices by JAX's collectives and lax.ppermute only.
A program may use at most 64 MiB of HBM per device.

v0:
```python
import jax
import jax.numpy as jnp
from jax import lax
from jax.experimental import pallas as pl
from jax.experimental.pallas import tpu as pltpu
from jax.sharding import PartitionSpec as P


DIRS = 6
SUB_ROW = 4
SUBS = 32
GROUPS = 16
BLOCK = 384
MODES = 128
MODES2 = 256
PACKED = BLOCK + MODES2
CHIPS = SUBS // 2
ROWS = MODES2 // SUBS

EXCHANGES = (("row", 0), ("row", 1), ("group", 0), ("group", 1), ("column", 1), ("column", 0))


F32 = jnp.float32
BF16 = jnp.bfloat16
SMEM = pl.BlockSpec(memory_space=pltpu.SMEM)
VMEM = pl.BlockSpec(memory_space=pltpu.VMEM)
HBM = pl.BlockSpec(memory_space=pltpu.HBM)


def swap_pairs(extent, odd):
    pairs = []
    for low in range(odd, extent - 1, 2):
        pairs += [(low, low + 1), (low + 1, low)]
    return pairs


def exchange(packed, kind, odd):
    if kind == "group":
        return lax.ppermute(packed, "group", swap_pairs(GROUPS, odd))
    pairs = []
    if kind == "row":
        for one, two in swap_pairs(SUBS // SUB_ROW, odd):
            pairs += [(one * SUB_ROW + c, two * SUB_ROW + c) for c in range(SUB_ROW)]
    else:
        for one, two in swap_pairs(SUB_ROW, odd):
            pairs += [(r * SUB_ROW + one, r * SUB_ROW + two) for r in range(SUBS // SUB_ROW)]
    return lax.ppermute(packed, "sub", pairs)


def slot_directions():
    sub, group = lax.axis_index("sub"), lax.axis_index("group")
    place = {
        "column": (lax.rem(sub, SUB_ROW), 0),
        "row": (lax.div(sub, SUB_ROW), 2),
        "group": (group, 4),
    }
    found = []
    for kind, odd in EXCHANGES:
        position, base = place[kind]
        found.append(base + 1 - lax.rem(position + odd, 2))
    return found


def split(x):
    high = x.astype(BF16)
    return high, (x - high.astype(F32)).astype(BF16)


def dot(a, b):
    return jnp.dot(a, b, preferred_element_type=F32)


def dot_wide(a, b):
    (a_high, a_low), (b_high, b_low) = a, b
    return dot(a_high, b_high) + (dot(a_high, b_low) + dot(a_low, b_high))


def dot_narrow(a, b_high, b_both):
    a_high, a_low = a
    both = dot(a_high, b_both)
    return both[:, :MODES] + (both[:, MODES:] + dot(a_low, b_high))


def pack_kernel(own_face, modes, basis, stiffness, *refs):
    outs, (near_modes, near_stiffness, faces, sems) = refs[:DIRS], refs[DIRS:]
    copies = [
        pltpu.make_async_copy(own_face, faces, sems.at[0]),
        pltpu.make_async_copy(modes, near_modes, sems.at[1]),
        pltpu.make_async_copy(stiffness, near_stiffness, sems.at[2]),
    ]
    for out in outs:
        for part in range(2):
            source = basis.at[:, part * MODES : (part + 1) * MODES]
            target = out.at[BLOCK + part * MODES : BLOCK + (part + 1) * MODES, :]
            copies.append(pltpu.make_async_copy(source, target, sems.at[len(copies)]))
    for copy in copies:
        copy.start()
    copies[0].wait()
    copies[1].wait()
    for direction, out in zip(slot_directions(), outs):
        first = pl.multiple_of(faces[0, direction] * BLOCK, BLOCK)
        out[:BLOCK, :] = near_modes[pl.ds(first, BLOCK), :]
    for copy in copies[2:]:
        copy.wait()


def self_kernel(modes, stiffness, self_block):
    high, low = split(modes[...])
    scaled = modes[...].T * stiffness[...]
    self_block[...] = dot_narrow(split(scaled), high, jnp.concatenate([high, low], axis=1))


def product_kernel(couplings, *refs):
    packed, (highs, lows) = refs[:DIRS], refs[DIRS:]
    for slot, direction in enumerate(slot_directions()):
        high, low = split(packed[slot][:BLOCK, :])
        both = jnp.concatenate([high, low], axis=1)
        product = dot_narrow(split(couplings[0, direction]), high, both)
        highs[slot], lows[slot] = split(product.T)


def half_kernel(present, highs, lows, self_block, own, *refs):
    fetched, (blocks, half, stack, others) = refs[:DIRS], refs[DIRS:]
    blocks[0, DIRS] = self_block[...]
    stack[:, :MODES] = self_block[...]
    others[:MODES, :MODES] = own[BLOCK : BLOCK + MODES, :]
    others[:MODES, MODES:] = own[BLOCK + MODES :, :]
    at = MODES
    for slot, direction in enumerate(slot_directions()):
        kind, _ = EXCHANGES[slot]
        got = fetched[slot]
        far_high, far_low = split(got[:BLOCK, :])
        both = jnp.concatenate([far_high, far_low], axis=1)
        weight = present[0, direction].astype(F32)
        block = dot_narrow((highs[slot], lows[slot]), far_high, both) * weight
        blocks[0, direction] = block
        if kind == "group":
            far = jnp.concatenate([got[BLOCK : BLOCK + MODES, :], got[BLOCK + MODES :, :]], axis=1)
            column = pl.multiple_of((direction - 4) * 2 * MODES2, MODES2)
            half[:, pl.ds(column, MODES2)] = dot_wide(split(block), split(far))
        else:
            stack[:, at : at + MODES] = block
            others[at : at + MODES, :MODES] = got[BLOCK : BLOCK + MODES, :]
            others[at : at + MODES, MODES:] = got[BLOCK + MODES :, :]
            at += MODES
    half[:, MODES2 : 2 * MODES2] = dot_wide(split(stack[...]), split(others[...]))


def term_kernel(own, partner, half, partner_half, near_blocks, terms, blocks, left, right, sem):
    copy = pltpu.make_async_copy(near_blocks, blocks, sem)
    copy.start()
    core = lax.rem(lax.axis_index("sub"), 2)
    for which, packed in enumerate((own, partner)):
        for part in range(2):
            piece = packed[BLOCK + part * MODES : BLOCK + (part + 1) * MODES, :]
            rows = piece.T.reshape(MODES // (2 * ROWS), 2, ROWS, MODES)
            chosen = jnp.where(core == 0, rows[:, 0], rows[:, 1]).reshape(MODES // 2, MODES)
            first = part * MODES // 2
            left[first : first + MODES // 2, which * MODES : (which + 1) * MODES] = chosen
    right[:MODES, :] = half[...]
    right[MODES:, :] = partner_half[...]
    terms[...] = dot_wide(split(left[...]), split(right[...])).reshape(terms.shape)
    copy.wait()


def sum_kernel(parts, out):
    total = parts[0]
    for other in range(1, CHIPS):
        total = total + parts[other]
    for which in range(3):
        out[0, which] = total[:, which * MODES2 : (which + 1) * MODES2]


def near(x):
    return pltpu.with_memory_space_constraint(x, pltpu.VMEM)


def far(x):
    return pltpu.with_memory_space_constraint(x, pltpu.HBM)


def call(kernel, ins, in_specs, outs, out_specs, scratch=(), flops=1_000_000):
    return pl.pallas_call(
        kernel,
        out_shape=outs,
        in_specs=in_specs,
        out_specs=out_specs,
        scratch_shapes=list(scratch),
        compiler_params=pltpu.CompilerParams(vmem_limit_bytes=16 << 20),
        cost_estimate=pl.CostEstimate(flops=flops, bytes_accessed=1_000_000, transcendentals=0),
    )(*ins)


def body(couplings, mode_rows, coarse_basis, stiffness, own_face, neighbour_face, present):
    *packed, modes, near_stiffness = call(
        pack_kernel,
        tuple(map(far, (own_face, mode_rows, coarse_basis, stiffness))),
        [HBM] * 4,
        [pltpu.VMEM((PACKED, MODES), F32)] * DIRS
        + [pltpu.VMEM(mode_rows.shape, F32), pltpu.VMEM(stiffness.shape, F32)],
        [VMEM] * (DIRS + 2),
        [pltpu.SMEM(own_face.shape, own_face.dtype), pltpu.SemaphoreType.DMA((3 + 2 * DIRS,))],
    )
    fetched = []
    for sent, (kind, odd) in zip(packed, EXCHANGES):
        fetched.append(near(exchange(sent, kind, odd)))
    (self_block,) = call(
        self_kernel,
        (modes, near_stiffness),
        [VMEM] * 2,
        [pltpu.VMEM((MODES, MODES), F32)],
        [VMEM],
        flops=4_000_000_000,
    )
    highs, lows = call(
        product_kernel,
        (near(couplings), *packed),
        [VMEM] * (1 + DIRS),
        [pltpu.VMEM((DIRS, MODES, BLOCK), BF16)] * 2,
        [VMEM] * 2,
        flops=800_000_000,
    )
    near_blocks, half = call(
        half_kernel,
        (present, highs, lows, self_block, packed[0], *fetched),
        [SMEM] + [VMEM] * (4 + DIRS),
        [pltpu.VMEM((1, DIRS + 1, MODES, MODES), F32), pltpu.VMEM((MODES, 3 * MODES2), F32)],
        [VMEM] * 2,
        [pltpu.VMEM((MODES, 5 * MODES), F32), pltpu.VMEM((5 * MODES, MODES2), F32)],
        flops=400_000_000,
    )
    partner_half = near(lax.ppermute(half, "sub", [(i, i ^ 1) for i in range(SUBS)]))
    terms, blocks = call(
        term_kernel,
        (packed[0], fetched[-1], half, partner_half, near_blocks),
        [VMEM] * 5,
        [
            pltpu.VMEM((CHIPS, ROWS, 3 * MODES2), F32),
            jax.ShapeDtypeStruct(near_blocks.shape, F32),
        ],
        [VMEM, HBM],
        [
            pltpu.VMEM((MODES, 2 * MODES), F32),
            pltpu.VMEM((2 * MODES, 3 * MODES2), F32),
            pltpu.SemaphoreType.DMA,
        ],
        flops=150_000_000,
    )
    chips = [[core + 2 * chip for chip in range(CHIPS)] for core in range(2)]
    parts = near(lax.all_to_all(terms, "sub", 0, 0, axis_index_groups=chips))
    (own_rows,) = call(
        sum_kernel, (parts,), [VMEM], [jax.ShapeDtypeStruct((1, 3, ROWS, MODES2), F32)], [VMEM]
    )
    return (blocks, own_rows)


def solution(mesh):
    both = ("group", "sub")
    return jax.shard_map(
        body,
        mesh=mesh,
        in_specs=(
            P(both, None, None, None),
            P(both, None),
            P(both, None),
            P(both, None),
            P(both, None),
            P(both, None),
            P(both, None),
        ),
        out_specs=(P(both, None, None, None), P("group", None, "sub", None)),
        check_vma=False,
    )
```

profile of v0, /device:TPU:96, one launch (start us, length us, event | category | flops | bytes accessed | tf_op | source)
XLA Modules:
  0.0 56.7 jit_solution(7755074770888178035)
XLA Ops:
  0.6 1.7 %shard_map.77 = (f32[640,128]{1,0:T(8,128)S(1)}, f32[640,128]{1,0:T(8,128)S(1)}, f32[640,128]{1,0:T(8,128)S(1)}, f32[640,128]{1,0:T(8,128)S(1)}, f32[640,128]{1,...) custom-call(s32[1,6]{1,0:T(1,128)} %own_face.1, f32[1536,128]{1,0:T(8,128)} %modes.1, ...), custom_call_target="tpu_custom_call" | custom-call | flops 1000000 | bytes 1000000 | tf_op jit(solution)/shard_map/pallas_call | solution.py:183
  2.4 5.1 %collective-permute-start.1 = (f32[640,128]{1,0:T(8,128)S(1)}, f32[640,128]{1,0:T(8,128)S(1)}, u32[]{:S(2)}, u32[]{:S(2)}) collective-permute-start(f32[640,128]{1,0:T(8,128)S(1)} %get-tuple-element.16.refs_0_.own), channel_id=1, source_target_pairs={{0,4},{1,5},{2,6},{3,7},{4,0},{5,1},{6,2},{7,3},{8,12},{9,13},{10,... | collective-permute-start | bytes 983048 | tf_op jit(solution)/shard_map/ppermute | solution.py:47
  7.5 1.9 %collective-permute-start = (f32[640,128]{1,0:T(8,128)S(1)}, f32[640,128]{1,0:T(8,128)S(1)}, u32[]{:S(2)}, u32[]{:S(2)}) collective-permute-start(f32[640,128]{1,0:T(8,128)S(1)} %get-tuple-element.17.refs_5_), channel_id=1, source_target_pairs={{0,1},{4,5},{8,9},{12,13},{16,17},{20,21},{24,25},{28,29},{1,0},{5... | collective-permute-start | bytes 983048 | tf_op jit(solution)/shard_map/ppermute | solution.py:47
  9.4 0.7 %collective-permute-start.2 = (f32[640,128]{1,0:T(8,128)S(1)}, f32[640,128]{1,0:T(8,128)S(1)}, u32[]{:S(2)}, u32[]{:S(2)}) collective-permute-start(f32[640,128]{1,0:T(8,128)S(1)} %get-tuple-element.18.refs_1_), channel_id=1, source_target_pairs={{4,8},{5,9},{6,10},{7,11},{8,4},{9,5},{10,6},{11,7},{12,16},{13,17... | collective-permute-start | bytes 983048 | tf_op jit(solution)/shard_map/ppermute | solution.py:47
  10.1 2.0 %collective-permute-start.3 = (f32[640,128]{1,0:T(8,128)S(1)}, f32[640,128]{1,0:T(8,128)S(1)}, u32[]{:S(2)}, u32[]{:S(2)}) collective-permute-start(f32[640,128]{1,0:T(8,128)S(1)} %get-tuple-element.19.refs_2_), channel_id=1, source_target_pairs={{0,32},{32,0},{64,96},{96,64},{128,160},{160,128},{192,224},{224,1... | collective-permute-start | bytes 983048 | tf_op jit(solution)/shard_map/ppermute | solution.py:39
  12.1 6.8 %collective-permute-start.4 = (f32[640,128]{1,0:T(8,128)S(1)}, f32[640,128]{1,0:T(8,128)S(1)}, u32[]{:S(2)}, u32[]{:S(2)}) collective-permute-start(f32[640,128]{1,0:T(8,128)S(1)} %get-tuple-element.20.refs_3_), channel_id=1, source_target_pairs={{32,64},{64,32},{96,128},{128,96},{160,192},{192,160},{224,256},{2... | collective-permute-start | bytes 983048 | tf_op jit(solution)/shard_map/ppermute | solution.py:39
  19.0 0.0 copy-start
  19.0 2.0 %copy-done = f32[1,6,384,384]{3,2,1,0:T(8,128)S(1)} copy-done((f32[1,6,384,384]{3,2,1,0:T(8,128)S(1)}, f32[1,6,384,384]{3,2,1,0:T(8,128)}, u32[]{:S(2)}) %copy-start) | copy-done | bytes 3538968
  21.0 1.3 %shard_map.78 = (bf16[6,128,384]{2,1,0:T(8,128)(2,1)S(1)}, bf16[6,128,384]{2,1,0:T(8,128)(2,1)S(1)}) custom-call(f32[1,6,384,384]{3,2,1,0:T(8,128)S(1)} %copy-done, f32[640,128]{1,0:T(8,128)S(1)} %get-tuple-element.16.refs_0_.own, f32[640,128]{1,0:T(8,128)S(1)} %get-tuple-element.18.refs_1_, f32[640,128]{1,0:T(8,128)S(1)} %get-tuple-element.19.refs_2_, ...), custom_call_target="tpu_custom_call" | custom-call | flops 800000000 | bytes 1000000 | tf_op jit(solution)/shard_map/pallas_call | solution.py:183
  22.3 0.0 collective-permute-done.1.refs_0_
  22.4 0.7 %collective-permute-start.5 = (f32[640,128]{1,0:T(8,128)S(1)}, f32[640,128]{1,0:T(8,128)S(1)}, u32[]{:S(2)}, u32[]{:S(2)}) collective-permute-start(f32[640,128]{1,0:T(8,128)S(1)} %get-tuple-element.21.refs_4_), channel_id=1, source_target_pairs={{1,2},{5,6},{9,10},{13,14},{17,18},{21,22},{25,26},{29,30},{2,1},{... | collective-permute-start | bytes 983048 | tf_op jit(solution)/shard_map/ppermute | solution.py:47
  23.0 0.0 copy-start.1
  23.1 0.4 shard_map.79.self_block
  23.5 0.0 collective-permute-done.refs_5_.partner
  23.5 0.0 collective-permute-done.2.refs_1_
  23.5 0.0 collective-permute-done.3.refs_2_
  23.5 3.6 %collective-permute-done.4.refs_3_ = f32[640,128]{1,0:T(8,128)S(1)} collective-permute-done((f32[640,128]{1,0:T(8,128)S(1)}, f32[640,128]{1,0:T(8,128)S(1)}, u32[]{:S(2)}, u32[]{:S(2)}) %collective-permute-start.4) | collective-permute-done | bytes 327712 | tf_op jit(solution)/shard_map/ppermute | solution.py:39
  27.1 0.0 collective-permute-done.5.refs_4_
  27.1 0.0 copy-done.1
  27.1 1.9 %shard_map.80 = (f32[1,7,128,128]{3,2,1,0:T(8,128)S(1)}, f32[128,768]{1,0:T(8,128)S(1)}) custom-call(s32[1,6]{1,0:T(1,128)S(1)} %copy-done.1, bf16[6,128,384]{2,1,0:T(8,128)(2,1)S(1)} %get-tuple-element.22.highs, bf16[6,128,384]{2,1,0:T(8,128)(2,1)S(1)} %get-tuple-element.23.lows, f32[128,128]{1,0:T(8,128)S(1)} %shard_map.79.self_block, ...), custom_call_target="tpu_custom_call" | custom-call | flops 400000000 | bytes 1000000 | tf_op jit(solution)/shard_map/pallas_call | solution.py:183
  29.0 5.5 %collective-permute-start.6 = (f32[128,768]{1,0:T(8,128)S(1)}, f32[128,768]{1,0:T(8,128)S(1)}, u32[]{:S(2)}, u32[]{:S(2)}) collective-permute-start(f32[128,768]{1,0:T(8,128)S(1)} %get-tuple-element.26.half), channel_id=1, source_target_pairs={{0,1},{1,0},{2,3},{3,2},{4,5},{5,4},{6,7},{7,6},{8,9},{9,8},{10,11... | collective-permute-start | bytes 1179656 | tf_op jit(solution)/shard_map/ppermute | solution.py:232
  34.5 1.3 %collective-permute-done.6.partner_half = f32[128,768]{1,0:T(8,128)S(1)} collective-permute-done((f32[128,768]{1,0:T(8,128)S(1)}, f32[128,768]{1,0:T(8,128)S(1)}, u32[]{:S(2)}, u32[]{:S(2)}) %collective-permute-start.6) | collective-permute-done | bytes 393248 | tf_op jit(solution)/shard_map/ppermute | solution.py:232
  35.8 0.8 %shard_map.81 = (f32[16,8,768]{2,1,0:T(8,128)S(1)}, f32[1,7,128,128]{3,2,1,0:T(8,128)}) custom-call(f32[640,128]{1,0:T(8,128)S(1)} %get-tuple-element.16.refs_0_.own, f32[640,128]{1,0:T(8,128)S(1)} %collective-permute-done.refs_5_.partner, f32[128,768]{1,0:T(8,128)S(1)} %get-tuple-element.26.half, f32[128,768]{1,0:T(8,128)S(1)} %collective-permute-done.6.partner_half, ...), custom_call_target="tpu_custom_call" | custom-call | flops 150000000 | bytes 1000000 | tf_op jit(solution)/shard_map/pallas_call | solution.py:183
  36.6 19.4 %all_to_all.5.parts = f32[16,8,768]{2,1,0:T(8,128)S(1)} all-to-all(f32[16,8,768]{2,1,0:T(8,128)S(1)} %get-tuple-element.29), channel_id=1, replica_groups={{0,2,4,6,8,10,12,14,16,18,20,22,24,26,28,30},{1,3,5,7,9,11,13,15,17,19,..., dimensions={0} | all-to-all | bytes 786432 | tf_op jit(solution)/shard_map/all_to_all | solution.py:250
  56.0 0.6 %shard_map.82 = f32[1,3,8,256]{3,2,1,0:T(8,128)} custom-call(f32[16,8,768]{2,1,0:T(8,128)S(1)} %all_to_all.5.parts), custom_call_target="tpu_custom_call" | custom-call | flops 1000000 | bytes 1000000 | tf_op jit(solution)/shard_map/pallas_call | solution.py:183
Async XLA Ops:
  2.4 20.0 %collective-permute-start.1 = (f32[640,128]{1,0:T(8,128)S(1)}, f32[640,128]{1,0:T(8,128)S(1)}, u32[]{:S(2)}, u32[]{:S(2)}) collective-permute-start(f32[640,128]{1,0:T(8,128)S(1)} %get-tuple-element.16.refs_0_.own), channel_id=1, source_target_pairs={{0,4},{1,5},{2,6},{3,7},{4,0},{5,1},{6,2},{7,3},{8,12},{9,13},{10,... | collective-permute-start | bytes 983048 | tf_op jit(solution)/shard_map/ppermute | solution.py:47
  7.5 16.0 %collective-permute-start = (f32[640,128]{1,0:T(8,128)S(1)}, f32[640,128]{1,0:T(8,128)S(1)}, u32[]{:S(2)}, u32[]{:S(2)}) collective-permute-start(f32[640,128]{1,0:T(8,128)S(1)} %get-tuple-element.17.refs_5_), channel_id=1, source_target_pairs={{0,1},{4,5},{8,9},{12,13},{16,17},{20,21},{24,25},{28,29},{1,0},{5... | collective-permute-start | bytes 983048 | tf_op jit(solution)/shard_map/ppermute | solution.py:47
  9.4 14.1 %collective-permute-start.2 = (f32[640,128]{1,0:T(8,128)S(1)}, f32[640,128]{1,0:T(8,128)S(1)}, u32[]{:S(2)}, u32[]{:S(2)}) collective-permute-start(f32[640,128]{1,0:T(8,128)S(1)} %get-tuple-element.18.refs_1_), channel_id=1, source_target_pairs={{4,8},{5,9},{6,10},{7,11},{8,4},{9,5},{10,6},{11,7},{12,16},{13,17... | collective-permute-start | bytes 983048 | tf_op jit(solution)/shard_map/ppermute | solution.py:47
  10.1 13.4 %collective-permute-start.3 = (f32[640,128]{1,0:T(8,128)S(1)}, f32[640,128]{1,0:T(8,128)S(1)}, u32[]{:S(2)}, u32[]{:S(2)}) collective-permute-start(f32[640,128]{1,0:T(8,128)S(1)} %get-tuple-element.19.refs_2_), channel_id=1, source_target_pairs={{0,32},{32,0},{64,96},{96,64},{128,160},{160,128},{192,224},{224,1... | collective-permute-start | bytes 983048 | tf_op jit(solution)/shard_map/ppermute | solution.py:39
  12.1 14.9 %collective-permute-start.4 = (f32[640,128]{1,0:T(8,128)S(1)}, f32[640,128]{1,0:T(8,128)S(1)}, u32[]{:S(2)}, u32[]{:S(2)}) collective-permute-start(f32[640,128]{1,0:T(8,128)S(1)} %get-tuple-element.20.refs_3_), channel_id=1, source_target_pairs={{32,64},{64,32},{96,128},{128,96},{160,192},{192,160},{224,256},{2... | collective-permute-start | bytes 983048 | tf_op jit(solution)/shard_map/ppermute | solution.py:39
  19.0 2.0 %copy-start = (f32[1,6,384,384]{3,2,1,0:T(8,128)S(1)}, f32[1,6,384,384]{3,2,1,0:T(8,128)}, u32[]{:S(2)}) copy-start(f32[1,6,384,384]{3,2,1,0:T(8,128)} %couplings.1) | copy-start | bytes 10616836
  22.4 4.7 %collective-permute-start.5 = (f32[640,128]{1,0:T(8,128)S(1)}, f32[640,128]{1,0:T(8,128)S(1)}, u32[]{:S(2)}, u32[]{:S(2)}) collective-permute-start(f32[640,128]{1,0:T(8,128)S(1)} %get-tuple-element.21.refs_4_), channel_id=1, source_target_pairs={{1,2},{5,6},{9,10},{13,14},{17,18},{21,22},{25,26},{29,30},{2,1},{... | collective-permute-start | bytes 983048 | tf_op jit(solution)/shard_map/ppermute | solution.py:47
  23.0 4.0 %copy-start.1 = (s32[1,6]{1,0:T(1,128)S(1)}, s32[1,6]{1,0:T(1,128)}, u32[]{:S(2)}) copy-start(s32[1,6]{1,0:T(1,128)} %present.1) | copy-start | bytes 76
  29.0 6.9 %collective-permute-start.6 = (f32[128,768]{1,0:T(8,128)S(1)}, f32[128,768]{1,0:T(8,128)S(1)}, u32[]{:S(2)}, u32[]{:S(2)}) collective-permute-start(f32[128,768]{1,0:T(8,128)S(1)} %get-tuple-element.26.half), channel_id=1, source_target_pairs={{0,1},{1,0},{2,3},{3,2},{4,5},{5,4},{6,7},{7,6},{8,9},{9,8},{10,11... | collective-permute-start | bytes 1179656 | tf_op jit(solution)/shard_map/ppermute | solution.py:232
where the time goes:
time: 57 us; the launch traced here: 56.7 us
  starting transfers between devices  22.8 us (40%)
  blocking collectives  19.4 us (34%)
  Pallas kernels  6.8 us (12%)
  waiting for transfers between devices  4.9 us (9%)
  local copies, waits for them, and re-layouts  2 us (4%)
  between operations  0.77 us (1%)
    all_to_all x1, blocking collectives, body(): parts = near(lax.all_to_all(terms, 'sub', 0, 0, axis_index_groups=chips))  19.4 us
    ppermute x2, starting transfers between devices, exchange(): return lax.ppermute(packed, 'group', swap_pairs(GROUPS, odd))  8.86 us
    ppermute x4, starting transfers between devices, exchange(): return lax.ppermute(packed, 'sub', pairs)  8.39 us
    pallas_call x6, Pallas kernels, call(): pl.pallas_call(kernel, out_shape=outs, in_specs=in_specs, out_specs=out_s...  6.8 us
    ppermute x1, starting transfers between devices, body(): lax.ppermute(half, 'sub', [(i, i ^ 1) for i in range(SUBS)])  5.52 us
    ppermute x2, waiting for transfers between devices, exchange(): return lax.ppermute(packed, 'group', swap_pairs(GROUPS, odd))  3.56 us
    unnamed x4, local copies, waits for them, and re-layouts  2 us
    ppermute x1, waiting for transfers between devices, body(): lax.ppermute(half, 'sub', [(i, i ^ 1) for i in range(SUBS)])  1.33 us
  transfers between devices with their start and end apart: 7, of which 2 were waited for; matrix products, arithmetic and copies ran while one was open for 0% of the time, Pallas kernels for 3%

commit v1 on v0

--- a/solution.py
+++ b/solution.py
@@ -17,7 +17,8 @@
 CHIPS = SUBS // 2
 ROWS = MODES2 // SUBS
 
-EXCHANGES = (("row", 0), ("row", 1), ("group", 0), ("group", 1), ("column", 1), ("column", 0))
+EXCHANGES = (("row", 1), ("row", 0), ("group", 0), ("group", 1), ("column", 1), ("column", 0))
+EARLY, LATE = (0, 2, 5), (1, 3, 4)
 
 
 F32 = jnp.float32
@@ -119,36 +120,57 @@
         highs[slot], lows[slot] = split(product.T)
 
 
-def half_kernel(present, highs, lows, self_block, own, *refs):
-    fetched, (blocks, half, stack, others) = refs[:DIRS], refs[DIRS:]
-    blocks[0, DIRS] = self_block[...]
+def coarse_block(present, highs, lows, got, slot, direction):
+    far_high, far_low = split(got[:BLOCK, :])
+    both = jnp.concatenate([far_high, far_low], axis=1)
+    weight = present[0, direction].astype(F32)
+    return dot_narrow((highs[slot], lows[slot]), far_high, both) * weight
+
+
+def half_terms(present, highs, lows, slots, fetched, blocks, stack, others, at):
+    directions = slot_directions()
+    for place, (slot, got) in enumerate(zip(slots, fetched)):
+        block = coarse_block(present, highs, lows, got, slot, directions[slot])
+        blocks[place] = block
+        low, high = got[BLOCK : BLOCK + MODES, :], got[BLOCK + MODES :, :]
+        if EXCHANGES[slot][0] == "group":
+            outer = dot_wide(split(block), split(jnp.concatenate([low, high], axis=1)))
+        else:
+            stack[:, at : at + MODES] = block
+            others[at : at + MODES, :MODES] = low
+            others[at : at + MODES, MODES:] = high
+            at += MODES
+    return outer, dot_wide(split(stack[...]), split(others[...]))
+
+
+def early_kernel(present, highs, lows, self_block, own, *refs):
+    fetched, (blocks, outer, within, stack, others) = refs[: len(EARLY)], refs[len(EARLY) :]
     stack[:, :MODES] = self_block[...]
     others[:MODES, :MODES] = own[BLOCK : BLOCK + MODES, :]
     others[:MODES, MODES:] = own[BLOCK + MODES :, :]
-    at = MODES
-    for slot, direction in enumerate(slot_directions()):
-        kind, _ = EXCHANGES[slot]
-        got = fetched[slot]
-        far_high, far_low = split(got[:BLOCK, :])
-        both = jnp.concatenate([far_high, far_low], axis=1)
-        weight = present[0, direction].astype(F32)
-        block = dot_narrow((highs[slot], lows[slot]), far_high, both) * weight
-        blocks[0, direction] = block
-        if kind == "group":
-            far = jnp.concatenate([got[BLOCK : BLOCK + MODES, :], got[BLOCK + MODES :, :]], axis=1)
-            column = pl.multiple_of((direction - 4) * 2 * MODES2, MODES2)
-            half[:, pl.ds(column, MODES2)] = dot_wide(split(block), split(far))
-        else:
-            stack[:, at : at + MODES] = block
-            others[at : at + MODES, :MODES] = got[BLOCK : BLOCK + MODES, :]
-            others[at : at + MODES, MODES:] = got[BLOCK + MODES :, :]
-            at += MODES
-    half[:, MODES2 : 2 * MODES2] = dot_wide(split(stack[...]), split(others[...]))
-
-
-def term_kernel(own, partner, half, partner_half, near_blocks, terms, blocks, left, right, sem):
-    copy = pltpu.make_async_copy(near_blocks, blocks, sem)
-    copy.start()
+    outer[...], within[...] = half_terms(
+        present, highs, lows, EARLY, fetched, blocks, stack, others, MODES
+    )
+
+
+def late_kernel(present, highs, lows, early_outer, early_within, *refs):
+    fetched, (blocks, half, stack, others) = refs[: len(LATE)], refs[len(LATE) :]
+    outer, within = half_terms(present, highs, lows, LATE, fetched, blocks, stack, others, 0)
+    half[:, MODES2 : 2 * MODES2] = within + early_within[...]
+    for slots, part in ((EARLY, early_outer[...]), (LATE, outer)):
+        (slot,) = [slot for slot in slots if EXCHANGES[slot][0] == "group"]
+        column = pl.multiple_of((slot_directions()[slot] - 4) * 2 * MODES2, MODES2)
+        half[:, pl.ds(column, MODES2)] = part
+
+
+def left_kernel(own, partner, half, self_block, early, late, left, terms, blocks, stack, sems):
+    copies = [pltpu.make_async_copy(self_block, blocks.at[0, DIRS], sems.at[DIRS])]
+    for slots, near_blocks in ((EARLY, early), (LATE, late)):
+        for place, slot in enumerate(slots):
+            target = blocks.at[0, slot_directions()[slot]]
+            copies.append(pltpu.make_async_copy(near_blocks.at[place], target, sems.at[slot]))
+    for copy in copies:
+        copy.start()
     core = lax.rem(lax.axis_index("sub"), 2)
     for which, packed in enumerate((own, partner)):
         for part in range(2):
@@ -156,11 +178,16 @@
             rows = piece.T.reshape(MODES // (2 * ROWS), 2, ROWS, MODES)
             chosen = jnp.where(core == 0, rows[:, 0], rows[:, 1]).reshape(MODES // 2, MODES)
             first = part * MODES // 2
-            left[first : first + MODES // 2, which * MODES : (which + 1) * MODES] = chosen
-    right[:MODES, :] = half[...]
-    right[MODES:, :] = partner_half[...]
-    terms[...] = dot_wide(split(left[...]), split(right[...])).reshape(terms.shape)
-    copy.wait()
+            stack[which, first : first + MODES // 2, :] = chosen
+    left[0], left[1] = split(stack[1])
+    terms[...] = dot_wide(split(stack[0]), split(half[...]))
+    for copy in copies:
+        copy.wait()
+
+
+def term_kernel(left, partner_half, own_terms, terms):
+    product = dot_wide((left[0], left[1]), split(partner_half[...]))
+    terms[...] = (own_terms[...] + product).reshape(terms.shape)
 
 
 def sum_kernel(parts, out):
@@ -220,30 +247,46 @@
         [VMEM] * 2,
         flops=800_000_000,
     )
-    near_blocks, half = call(
-        half_kernel,
-        (present, highs, lows, self_block, packed[0], *fetched),
-        [SMEM] + [VMEM] * (4 + DIRS),
-        [pltpu.VMEM((1, DIRS + 1, MODES, MODES), F32), pltpu.VMEM((MODES, 3 * MODES2), F32)],
+    block_shape, half_shape = (MODES, MODES), (MODES, MODES2)
+    early_blocks, early_outer, early_within = call(
+        early_kernel,
+        (present, highs, lows, self_block, packed[0], *[fetched[slot] for slot in EARLY]),
+        [SMEM] + [VMEM] * (4 + len(EARLY)),
+        [pltpu.VMEM((len(EARLY), *block_shape), F32)] + [pltpu.VMEM(half_shape, F32)] * 2,
+        [VMEM] * 3,
+        [pltpu.VMEM((MODES, 3 * MODES), F32), pltpu.VMEM((3 * MODES, MODES2), F32)],
+        flops=200_000_000,
+    )
+    late_blocks, half = call(
+        late_kernel,
+        (present, highs, lows, early_outer, early_within, *[fetched[slot] for slot in LATE]),
+        [SMEM] + [VMEM] * (4 + len(LATE)),
+        [pltpu.VMEM((len(LATE), *block_shape), F32), pltpu.VMEM((MODES, 3 * MODES2), F32)],
         [VMEM] * 2,
-        [pltpu.VMEM((MODES, 5 * MODES), F32), pltpu.VMEM((5 * MODES, MODES2), F32)],
-        flops=400_000_000,
+        [pltpu.VMEM((MODES, 2 * MODES), F32), pltpu.VMEM((2 * MODES, MODES2), F32)],
+        flops=200_000_000,
     )
     partner_half = near(lax.ppermute(half, "sub", [(i, i ^ 1) for i in range(SUBS)]))
-    terms, blocks = call(
+    partner = fetched[EXCHANGES.index(("column", 0))]
+    left, own_terms, blocks = call(
+        left_kernel,
+        (packed[0], partner, half, self_block, early_blocks, late_blocks),
+        [VMEM] * 6,
+        [
+            pltpu.VMEM((2, MODES, MODES), BF16),
+            pltpu.VMEM((MODES, 3 * MODES2), F32),
+            jax.ShapeDtypeStruct((1, DIRS + 1, MODES, MODES), F32),
+        ],
+        [VMEM, VMEM, HBM],
+        [pltpu.VMEM((2, MODES, MODES), F32), pltpu.SemaphoreType.DMA((DIRS + 1,))],
+        flops=150_000_000,
+    )
+    (terms,) = call(
         term_kernel,
-        (packed[0], fetched[-1], half, partner_half, near_blocks),
-        [VMEM] * 5,
-        [
-            pltpu.VMEM((CHIPS, ROWS, 3 * MODES2), F32),
-            jax.ShapeDtypeStruct(near_blocks.shape, F32),
-        ],
-        [VMEM, HBM],
-        [
-            pltpu.VMEM((MODES, 2 * MODES), F32),
-            pltpu.VMEM((2 * MODES, 3 * MODES2), F32),
-            pltpu.SemaphoreType.DMA,
-        ],
+        (left, partner_half, own_terms),
+        [VMEM] * 3,
+        [pltpu.VMEM((CHIPS, ROWS, 3 * MODES2), F32)],
+        [VMEM],
         flops=150_000_000,
     )
     chips = [[core + 2 * chip for chip in range(CHIPS)] for core in range(2)]

time: 57 us -> 55.4 us (0.972)
  blocking collectives: 19.4 us -> 16.3 us
  waiting for transfers between devices: 4.9 us -> 1.89 us
  starting transfers between devices: 22.8 us -> 25.6 us
  Pallas kernels: 6.8 us -> 8.29 us
    all_to_all x1, blocking collectives: 19.4 us -> 16.3 us  [body(): parts = near(lax.all_to_all(terms, 'sub', 0, 0, axis_index_groups=chips))]
    ppermute x4, starting transfers between devices: 8.39 us -> 10.9 us  [exchange(): return lax.ppermute(packed, 'sub', pairs)]
    ppermute x2, waiting for transfers between devices: 3.56 us -> 1.67 us  [exchange(): return lax.ppermute(packed, 'group', swap_pairs(GROUPS, odd))]
    pallas_call x6 -> x8, Pallas kernels: 6.8 us -> 8.29 us  [call(): pl.pallas_call(kernel, out_shape=outs, in_specs=in_specs, out_specs=out_s...]
    ppermute x1, waiting for transfers between devices: 1.33 us -> 0.21 us  [body(): lax.ppermute(half, 'sub', [(i, i ^ 1) for i in range(SUBS)])]
  transfers between devices with their start and end apart: 7 -> 7, of which waited for: 2 -> 2; matrix products, arithmetic and copies ran while one was open for 0% -> 0% of each run, Pallas kernels for 3% -> 8%
where the time goes in v1:
time: 55.4 us; the launch traced here: 55 us
  starting transfers between devices  25.6 us (46%)
  blocking collectives  16.3 us (29%)
  Pallas kernels  8.29 us (15%)
  local copies, waits for them, and re-layouts  2.2 us (4%)
  waiting for transfers between devices  1.89 us (3%)
  between operations  0.78 us (1%)
    all_to_all x1, blocking collectives, body(): parts = near(lax.all_to_all(terms, 'sub', 0, 0, axis_index_groups=chips))  16.3 us
    ppermute x4, starting transfers between devices, exchange(): return lax.ppermute(packed, 'sub', pairs)  10.9 us
    ppermute x2, starting transfers between devices, exchange(): return lax.ppermute(packed, 'group', swap_pairs(GROUPS, odd))  8.86 us
    pallas_call x8, Pallas kernels, call(): pl.pallas_call(kernel, out_shape=outs, in_specs=in_specs, out_specs=out_s...  8.29 us
    ppermute x1, starting transfers between devices, body(): lax.ppermute(half, 'sub', [(i, i ^ 1) for i in range(SUBS)])  5.82 us
    unnamed x4, local copies, waits for them, and re-layouts  2.2 us
    ppermute x2, waiting for transfers between devices, exchange(): return lax.ppermute(packed, 'group', swap_pairs(GROUPS, odd))  1.67 us
  transfers between devices with their start and end apart: 7, of which 2 were waited for; matrix products, arithmetic and copies ran while one was open for 0% of the time, Pallas kernels for 8%

profile of v1, /device:TPU:96, one launch (start us, length us, event | category | flops | bytes accessed | tf_op | source)
XLA Modules:
  0.0 55.0 jit_solution(6477218267256050789)
XLA Ops:
  0.6 1.7 %shard_map.77 = (f32[640,128]{1,0:T(8,128)S(1)}, f32[640,128]{1,0:T(8,128)S(1)}, f32[640,128]{1,0:T(8,128)S(1)}, f32[640,128]{1,0:T(8,128)S(1)}, f32[640,128]{1,...) custom-call(s32[1,6]{1,0:T(1,128)} %own_face.1, f32[1536,128]{1,0:T(8,128)} %modes.1, ...), custom_call_target="tpu_custom_call" | custom-call | flops 1000000 | bytes 1000000 | tf_op jit(solution)/shard_map/pallas_call | solution.py:210
  2.4 0.7 %collective-permute-start.1 = (f32[640,128]{1,0:T(8,128)S(1)}, f32[640,128]{1,0:T(8,128)S(1)}, u32[]{:S(2)}, u32[]{:S(2)}) collective-permute-start(f32[640,128]{1,0:T(8,128)S(1)} %get-tuple-element.20.refs_0_.own), channel_id=1, source_target_pairs={{4,8},{5,9},{6,10},{7,11},{8,4},{9,5},{10,6},{11,7},{12,16},{13,17... | collective-permute-start | bytes 983048 | tf_op jit(solution)/shard_map/ppermute | solution.py:48
  3.1 1.9 %collective-permute-start = (f32[640,128]{1,0:T(8,128)S(1)}, f32[640,128]{1,0:T(8,128)S(1)}, u32[]{:S(2)}, u32[]{:S(2)}) collective-permute-start(f32[640,128]{1,0:T(8,128)S(1)} %get-tuple-element.21.refs_5_), channel_id=1, source_target_pairs={{0,1},{4,5},{8,9},{12,13},{16,17},{20,21},{24,25},{28,29},{1,0},{5... | collective-permute-start | bytes 983048 | tf_op jit(solution)/shard_map/ppermute | solution.py:48
  5.0 2.0 %collective-permute-start.2 = (f32[640,128]{1,0:T(8,128)S(1)}, f32[640,128]{1,0:T(8,128)S(1)}, u32[]{:S(2)}, u32[]{:S(2)}) collective-permute-start(f32[640,128]{1,0:T(8,128)S(1)} %get-tuple-element.23.refs_2_), channel_id=1, source_target_pairs={{0,32},{32,0},{64,96},{96,64},{128,160},{160,128},{192,224},{224,1... | collective-permute-start | bytes 983048 | tf_op jit(solution)/shard_map/ppermute | solution.py:40
  7.0 7.6 %collective-permute-start.3 = (f32[640,128]{1,0:T(8,128)S(1)}, f32[640,128]{1,0:T(8,128)S(1)}, u32[]{:S(2)}, u32[]{:S(2)}) collective-permute-start(f32[640,128]{1,0:T(8,128)S(1)} %get-tuple-element.22.refs_1_), channel_id=1, source_target_pairs={{0,4},{1,5},{2,6},{3,7},{4,0},{5,1},{6,2},{7,3},{8,12},{9,13},{10,... | collective-permute-start | bytes 983048 | tf_op jit(solution)/shard_map/ppermute | solution.py:48
  14.6 6.8 %collective-permute-start.4 = (f32[640,128]{1,0:T(8,128)S(1)}, f32[640,128]{1,0:T(8,128)S(1)}, u32[]{:S(2)}, u32[]{:S(2)}) collective-permute-start(f32[640,128]{1,0:T(8,128)S(1)} %get-tuple-element.24.refs_3_), channel_id=1, source_target_pairs={{32,64},{64,32},{96,128},{128,96},{160,192},{192,160},{224,256},{2... | collective-permute-start | bytes 983048 | tf_op jit(solution)/shard_map/ppermute | solution.py:40
  21.5 0.0 copy-start
  21.5 2.0 %copy-done = f32[1,6,384,384]{3,2,1,0:T(8,128)S(1)} copy-done((f32[1,6,384,384]{3,2,1,0:T(8,128)S(1)}, f32[1,6,384,384]{3,2,1,0:T(8,128)}, u32[]{:S(2)}) %copy-start) | copy-done | bytes 3538968
  23.5 1.3 %shard_map.78 = (bf16[6,128,384]{2,1,0:T(8,128)(2,1)S(1)}, bf16[6,128,384]{2,1,0:T(8,128)(2,1)S(1)}) custom-call(f32[1,6,384,384]{3,2,1,0:T(8,128)S(1)} %copy-done, f32[640,128]{1,0:T(8,128)S(1)} %get-tuple-element.20.refs_0_.own, f32[640,128]{1,0:T(8,128)S(1)} %get-tuple-element.22.refs_1_, f32[640,128]{1,0:T(8,128)S(1)} %get-tuple-element.23.refs_2_, ...), custom_call_target="tpu_custom_call" | custom-call | flops 800000000 | bytes 1000000 | tf_op jit(solution)/shard_map/pallas_call | solution.py:210
  24.8 0.0 collective-permute-done.1.refs_0_
  24.8 0.7 %collective-permute-start.5 = (f32[640,128]{1,0:T(8,128)S(1)}, f32[640,128]{1,0:T(8,128)S(1)}, u32[]{:S(2)}, u32[]{:S(2)}) collective-permute-start(f32[640,128]{1,0:T(8,128)S(1)} %get-tuple-element.25.refs_4_), channel_id=1, source_target_pairs={{1,2},{5,6},{9,10},{13,14},{17,18},{21,22},{25,26},{29,30},{2,1},{... | collective-permute-start | bytes 983048 | tf_op jit(solution)/shard_map/ppermute | solution.py:48
  25.5 0.0 copy-start.1
  25.5 0.4 shard_map.79.self_block
  26.0 0.0 collective-permute-done.refs_2_.partner
  26.0 0.0 collective-permute-done.2.refs_1_
  26.0 0.2 copy-done.1
  26.2 1.4 %shard_map.80 = (f32[3,128,128]{2,1,0:T(8,128)S(1)}, f32[128,256]{1,0:T(8,128)S(1)}, f32[128,256]{1,0:T(8,128)S(1)}) custom-call(s32[1,6]{1,0:T(1,128)S(1)} %copy-done.1, bf16[6,128,384]{2,1,0:T(8,128)(2,1)S(1)} %get-tuple-element.26.highs, bf16[6,128,384]{2,1,0:T(8,128)(2,1)S(1)} %get-tuple-element.27.lows, f32[128,128]{1,0:T(8,128)S(1)} %shard_map.79.self_block, ...), custom_call_target="tpu_custom_call" | custom-call | flops 200000000 | bytes 1000000 | tf_op jit(solution)/shard_map/pallas_call | solution.py:210
  27.6 0.0 collective-permute-done.3.refs_0_
  27.6 1.7 %collective-permute-done.4.refs_1_ = f32[640,128]{1,0:T(8,128)S(1)} collective-permute-done((f32[640,128]{1,0:T(8,128)S(1)}, f32[640,128]{1,0:T(8,128)S(1)}, u32[]{:S(2)}, u32[]{:S(2)}) %collective-permute-start.4) | collective-permute-done | bytes 327712 | tf_op jit(solution)/shard_map/ppermute | solution.py:40
  29.3 0.0 collective-permute-done.5.refs_2_
  29.3 1.3 %shard_map.81 = (f32[3,128,128]{2,1,0:T(8,128)S(1)}, f32[128,768]{1,0:T(8,128)S(1)}) custom-call(s32[1,6]{1,0:T(1,128)S(1)} %copy-done.1, bf16[6,128,384]{2,1,0:T(8,128)(2,1)S(1)} %get-tuple-element.26.highs, bf16[6,128,384]{2,1,0:T(8,128)(2,1)S(1)} %get-tuple-element.27.lows, f32[128,256]{1,0:T(8,128)S(1)} %get-tuple-element.30.early_outer, ...), custom_call_target="tpu_custom_call" | custom-call | flops 200000000 | bytes 1000000 | tf_op jit(solution)/shard_map/pallas_call | solution.py:210
  30.6 5.8 %collective-permute-start.6 = (f32[128,768]{1,0:T(8,128)S(1)}, f32[128,768]{1,0:T(8,128)S(1)}, u32[]{:S(2)}, u32[]{:S(2)}) collective-permute-start(f32[128,768]{1,0:T(8,128)S(1)} %get-tuple-element.32.half), channel_id=1, source_target_pairs={{0,1},{1,0},{2,3},{3,2},{4,5},{5,4},{6,7},{7,6},{8,9},{9,8},{10,11... | collective-permute-start | bytes 1179656 | tf_op jit(solution)/shard_map/ppermute | solution.py:269
  36.4 1.1 %shard_map.82 = (bf16[2,128,128]{2,1,0:T(8,128)(2,1)S(1)}, f32[128,768]{1,0:T(8,128)S(1)}, f32[1,7,128,128]{3,2,1,0:T(8,128)}) custom-call(f32[640,128]{1,0:T(8,128)S(1)} %get-tuple-element.20.refs_0_.own, f32[640,128]{1,0:T(8,128)S(1)} %collective-permute-done.refs_2_.partner, f32[128,768]{1,0:T(8,128)S(1)} %get-tuple-element.32.half, ...), custom_call_target="tpu_custom_call" | custom-call | flops 150000000 | bytes 1000000 | tf_op jit(solution)/shard_map/pallas_call | solution.py:210
  37.5 0.2 collective-permute-done.6.partner_half
  37.8 0.3 shard_map.83
  38.1 16.3 %all_to_all.5.parts = f32[16,8,768]{2,1,0:T(8,128)S(1)} all-to-all(f32[16,8,768]{2,1,0:T(8,128)S(1)} %shard_map.83), channel_id=1, replica_groups={{0,2,4,6,8,10,12,14,16,18,20,22,24,26,28,30},{1,3,5,7,9,11,13,15,17,19,..., dimensions={0} | all-to-all | bytes 786432 | tf_op jit(solution)/shard_map/all_to_all | solution.py:293
  54.3 0.6 %shard_map.84 = f32[1,3,8,256]{3,2,1,0:T(8,128)} custom-call(f32[16,8,768]{2,1,0:T(8,128)S(1)} %all_to_all.5.parts), custom_call_target="tpu_custom_call" | custom-call | flops 1000000 | bytes 1000000 | tf_op jit(solution)/shard_map/pallas_call | solution.py:210
Async XLA Ops:
  2.4 22.4 %collective-permute-start.1 = (f32[640,128]{1,0:T(8,128)S(1)}, f32[640,128]{1,0:T(8,128)S(1)}, u32[]{:S(2)}, u32[]{:S(2)}) collective-permute-start(f32[640,128]{1,0:T(8,128)S(1)} %get-tuple-element.20.refs_0_.own), channel_id=1, source_target_pairs={{4,8},{5,9},{6,10},{7,11},{8,4},{9,5},{10,6},{11,7},{12,16},{13,17... | collective-permute-start | bytes 983048 | tf_op jit(solution)/shard_map/ppermute | solution.py:48
  3.1 22.9 %collective-permute-start = (f32[640,128]{1,0:T(8,128)S(1)}, f32[640,128]{1,0:T(8,128)S(1)}, u32[]{:S(2)}, u32[]{:S(2)}) collective-permute-start(f32[640,128]{1,0:T(8,128)S(1)} %get-tuple-element.21.refs_5_), channel_id=1, source_target_pairs={{0,1},{4,5},{8,9},{12,13},{16,17},{20,21},{24,25},{28,29},{1,0},{5... | collective-permute-start | bytes 983048 | tf_op jit(solution)/shard_map/ppermute | solution.py:48
  5.0 21.0 %collective-permute-start.2 = (f32[640,128]{1,0:T(8,128)S(1)}, f32[640,128]{1,0:T(8,128)S(1)}, u32[]{:S(2)}, u32[]{:S(2)}) collective-permute-start(f32[640,128]{1,0:T(8,128)S(1)} %get-tuple-element.23.refs_2_), channel_id=1, source_target_pairs={{0,32},{32,0},{64,96},{96,64},{128,160},{160,128},{192,224},{224,1... | collective-permute-start | bytes 983048 | tf_op jit(solution)/shard_map/ppermute | solution.py:40
  7.0 20.6 %collective-permute-start.3 = (f32[640,128]{1,0:T(8,128)S(1)}, f32[640,128]{1,0:T(8,128)S(1)}, u32[]{:S(2)}, u32[]{:S(2)}) collective-permute-start(f32[640,128]{1,0:T(8,128)S(1)} %get-tuple-element.22.refs_1_), channel_id=1, source_target_pairs={{0,4},{1,5},{2,6},{3,7},{4,0},{5,1},{6,2},{7,3},{8,12},{9,13},{10,... | collective-permute-start | bytes 983048 | tf_op jit(solution)/shard_map/ppermute | solution.py:48
  14.6 14.7 %collective-permute-start.4 = (f32[640,128]{1,0:T(8,128)S(1)}, f32[640,128]{1,0:T(8,128)S(1)}, u32[]{:S(2)}, u32[]{:S(2)}) collective-permute-start(f32[640,128]{1,0:T(8,128)S(1)} %get-tuple-element.24.refs_3_), channel_id=1, source_target_pairs={{32,64},{64,32},{96,128},{128,96},{160,192},{192,160},{224,256},{2... | collective-permute-start | bytes 983048 | tf_op jit(solution)/shard_map/ppermute | solution.py:40
  21.5 2.0 %copy-start = (f32[1,6,384,384]{3,2,1,0:T(8,128)S(1)}, f32[1,6,384,384]{3,2,1,0:T(8,128)}, u32[]{:S(2)}) copy-start(f32[1,6,384,384]{3,2,1,0:T(8,128)} %couplings.1) | copy-start | bytes 10616836
  24.8 4.4 %collective-permute-start.5 = (f32[640,128]{1,0:T(8,128)S(1)}, f32[640,128]{1,0:T(8,128)S(1)}, u32[]{:S(2)}, u32[]{:S(2)}) collective-permute-start(f32[640,128]{1,0:T(8,128)S(1)} %get-tuple-element.25.refs_4_), channel_id=1, source_target_pairs={{1,2},{5,6},{9,10},{13,14},{17,18},{21,22},{25,26},{29,30},{2,1},{... | collective-permute-start | bytes 983048 | tf_op jit(solution)/shard_map/ppermute | solution.py:48
  25.5 0.7 %copy-start.1 = (s32[1,6]{1,0:T(1,128)S(1)}, s32[1,6]{1,0:T(1,128)}, u32[]{:S(2)}) copy-start(s32[1,6]{1,0:T(1,128)} %present.3) | copy-start | bytes 76
  30.6 7.2 %collective-permute-start.6 = (f32[128,768]{1,0:T(8,128)S(1)}, f32[128,768]{1,0:T(8,128)S(1)}, u32[]{:S(2)}, u32[]{:S(2)}) collective-permute-start(f32[128,768]{1,0:T(8,128)S(1)} %get-tuple-element.32.half), channel_id=1, source_target_pairs={{0,1},{1,0},{2,3},{3,2},{4,5},{5,4},{6,7},{7,6},{8,9},{9,8},{10,11... | collective-permute-start | bytes 1179656 | tf_op jit(solution)/shard_map/ppermute | solution.py:269

commit v2 on v1

--- a/solution.py
+++ b/solution.py
@@ -73,7 +73,16 @@
 
 def dot_wide(a, b):
     (a_high, a_low), (b_high, b_low) = a, b
-    return dot(a_high, b_high) + (dot(a_high, b_low) + dot(a_low, b_high))
+    count = a_high.shape[0]
+    tall = dot(jnp.concatenate([a_high, a_low], axis=0), b_high)
+    return tall[:count] + (tall[count:] + dot(a_high, b_low))
+
+
+def dot_stacked(a, b_both):
+    a_high, a_low = a
+    count = a_high.shape[0]
+    tall = dot(jnp.concatenate([a_high, a_low], axis=0), b_both)
+    return tall[:count, :MODES] + (tall[:count, MODES:] + tall[count:, :MODES])
 
 
 def dot_narrow(a, b_high, b_both):
@@ -105,14 +114,15 @@
         copy.wait()
 
 
-def self_kernel(modes, stiffness, self_block):
+def marker_kernel(marker):
+    marker[...] = jnp.zeros_like(marker)
+
+
+def product_kernel(couplings, modes, stiffness, marker, *refs):
+    packed, (highs, lows, self_block) = refs[:DIRS], refs[DIRS:]
     high, low = split(modes[...])
     scaled = modes[...].T * stiffness[...]
     self_block[...] = dot_narrow(split(scaled), high, jnp.concatenate([high, low], axis=1))
-
-
-def product_kernel(couplings, *refs):
-    packed, (highs, lows) = refs[:DIRS], refs[DIRS:]
     for slot, direction in enumerate(slot_directions()):
         high, low = split(packed[slot][:BLOCK, :])
         both = jnp.concatenate([high, low], axis=1)
@@ -124,7 +134,7 @@
     far_high, far_low = split(got[:BLOCK, :])
     both = jnp.concatenate([far_high, far_low], axis=1)
     weight = present[0, direction].astype(F32)
-    return dot_narrow((highs[slot], lows[slot]), far_high, both) * weight
+    return dot_stacked((highs[slot], lows[slot]), both) * weight
 
 
 def half_terms(present, highs, lows, slots, fetched, blocks, stack, others, at):
@@ -231,20 +241,15 @@
     fetched = []
     for sent, (kind, odd) in zip(packed, EXCHANGES):
         fetched.append(near(exchange(sent, kind, odd)))
-    (self_block,) = call(
-        self_kernel,
-        (modes, near_stiffness),
-        [VMEM] * 2,
-        [pltpu.VMEM((MODES, MODES), F32)],
-        [VMEM],
-        flops=4_000_000_000,
-    )
-    highs, lows = call(
+    (marker,) = call(
+        marker_kernel, (), [], [pltpu.VMEM((8, MODES), F32)], [VMEM], flops=4_000_000_000
+    )
+    highs, lows, self_block = call(
         product_kernel,
-        (near(couplings), *packed),
-        [VMEM] * (1 + DIRS),
-        [pltpu.VMEM((DIRS, MODES, BLOCK), BF16)] * 2,
-        [VMEM] * 2,
+        (near(couplings), modes, near_stiffness, marker, *packed),
+        [VMEM] * (4 + DIRS),
+        [pltpu.VMEM((DIRS, MODES, BLOCK), BF16)] * 2 + [pltpu.VMEM((MODES, MODES), F32)],
+        [VMEM] * 3,
         flops=800_000_000,
     )
     block_shape, half_shape = (MODES, MODES), (MODES, MODES2)
@@ -254,7 +259,10 @@
         [SMEM] + [VMEM] * (4 + len(EARLY)),
         [pltpu.VMEM((len(EARLY), *block_shape), F32)] + [pltpu.VMEM(half_shape, F32)] * 2,
         [VMEM] * 3,
-        [pltpu.VMEM((MODES, 3 * MODES), F32), pltpu.VMEM((3 * MODES, MODES2), F32)],
+        [
+            pltpu.VMEM((MODES, len(EARLY) * MODES), F32),
+            pltpu.VMEM((len(EARLY) * MODES, MODES2), F32),
+        ],
         flops=200_000_000,
     )
     late_blocks, half = call(
@@ -263,7 +271,10 @@
         [SMEM] + [VMEM] * (4 + len(LATE)),
         [pltpu.VMEM((len(LATE), *block_shape), F32), pltpu.VMEM((MODES, 3 * MODES2), F32)],
         [VMEM] * 2,
-        [pltpu.VMEM((MODES, 2 * MODES), F32), pltpu.VMEM((2 * MODES, MODES2), F32)],
+        [
+            pltpu.VMEM((MODES, (len(LATE) - 1) * MODES), F32),
+            pltpu.VMEM(((len(LATE) - 1) * MODES, MODES2), F32),
+        ],
         flops=200_000_000,
     )
     partner_half = near(lax.ppermute(half, "sub", [(i, i ^ 1) for i in range(SUBS)]))

time: 55.4 us -> 52.1 us (0.940)
  starting transfers between devices: 25.6 us -> 22.6 us
  waiting for transfers between devices: 1.89 us -> 3.04 us
  local copies, waits for them, and re-layouts: 2.2 us -> 1.16 us
    ppermute x1, starting transfers between devices: 5.82 us -> 2.74 us  [body(): lax.ppermute(half, 'sub', [(i, i ^ 1) for i in range(SUBS)])]
    ppermute x2, waiting for transfers between devices: 1.67 us -> 2.82 us  [exchange(): return lax.ppermute(packed, 'group', swap_pairs(GROUPS, odd))]
    unnamed x4, local copies, waits for them, and re-layouts: 2.2 us -> 1.16 us
where the time goes in v2:
time: 52.1 us; the launch traced here: 51.8 us
  starting transfers between devices  22.6 us (43%)
  blocking collectives  16.3 us (31%)
  Pallas kernels  7.93 us (15%)
  waiting for transfers between devices  3.04 us (6%)
  local copies, waits for them, and re-layouts  1.16 us (2%)
  between operations  0.79 us (2%)
    all_to_all x1, blocking collectives, body(): parts = near(lax.all_to_all(terms, 'sub', 0, 0, axis_index_groups=chips))  16.3 us
    ppermute x4, starting transfers between devices, exchange(): return lax.ppermute(packed, 'sub', pairs)  11 us
    ppermute x2, starting transfers between devices, exchange(): return lax.ppermute(packed, 'group', swap_pairs(GROUPS, odd))  8.86 us
    pallas_call x8, Pallas kernels, call(): pl.pallas_call(kernel, out_shape=outs, in_specs=in_specs, out_specs=out_s...  7.93 us
    ppermute x2, waiting for transfers between devices, exchange(): return lax.ppermute(packed, 'group', swap_pairs(GROUPS, odd))  2.82 us
    ppermute x1, starting transfers between devices, body(): lax.ppermute(half, 'sub', [(i, i ^ 1) for i in range(SUBS)])  2.74 us
    unnamed x4, local copies, waits for them, and re-layouts  1.16 us
  transfers between devices with their start and end apart: 7, of which 2 were waited for; matrix products, arithmetic and copies ran while one was open for 0% of the time, Pallas kernels for 8%

profile of v2, /device:TPU:96, one launch (start us, length us, event | category | flops | bytes accessed | tf_op | source)
XLA Modules:
  0.0 51.8 jit_solution(5509565286258622792)
XLA Ops:
  0.6 1.7 %shard_map.77 = (f32[640,128]{1,0:T(8,128)S(1)}, f32[640,128]{1,0:T(8,128)S(1)}, f32[640,128]{1,0:T(8,128)S(1)}, f32[640,128]{1,0:T(8,128)S(1)}, f32[640,128]{1,...) custom-call(s32[1,6]{1,0:T(1,128)} %own_face.1, f32[1536,128]{1,0:T(8,128)} %modes.1, ...), custom_call_target="tpu_custom_call" | custom-call | flops 1000000 | bytes 1000000 | tf_op jit(solution)/shard_map/pallas_call | solution.py:220
  2.4 0.7 %collective-permute-start.1 = (f32[640,128]{1,0:T(8,128)S(1)}, f32[640,128]{1,0:T(8,128)S(1)}, u32[]{:S(2)}, u32[]{:S(2)}) collective-permute-start(f32[640,128]{1,0:T(8,128)S(1)} %get-tuple-element.21.refs_0_.own), channel_id=1, source_target_pairs={{4,8},{5,9},{6,10},{7,11},{8,4},{9,5},{10,6},{11,7},{12,16},{13,17... | collective-permute-start | bytes 983048 | tf_op jit(solution)/shard_map/ppermute | solution.py:48
  3.1 1.9 %collective-permute-start = (f32[640,128]{1,0:T(8,128)S(1)}, f32[640,128]{1,0:T(8,128)S(1)}, u32[]{:S(2)}, u32[]{:S(2)}) collective-permute-start(f32[640,128]{1,0:T(8,128)S(1)} %get-tuple-element.22.refs_5_), channel_id=1, source_target_pairs={{0,1},{4,5},{8,9},{12,13},{16,17},{20,21},{24,25},{28,29},{1,0},{5... | collective-permute-start | bytes 983048 | tf_op jit(solution)/shard_map/ppermute | solution.py:48
  5.0 2.0 %collective-permute-start.2 = (f32[640,128]{1,0:T(8,128)S(1)}, f32[640,128]{1,0:T(8,128)S(1)}, u32[]{:S(2)}, u32[]{:S(2)}) collective-permute-start(f32[640,128]{1,0:T(8,128)S(1)} %get-tuple-element.26.refs_2_), channel_id=1, source_target_pairs={{0,32},{32,0},{64,96},{96,64},{128,160},{160,128},{192,224},{224,1... | collective-permute-start | bytes 983048 | tf_op jit(solution)/shard_map/ppermute | solution.py:40
  7.0 7.6 %collective-permute-start.3 = (f32[640,128]{1,0:T(8,128)S(1)}, f32[640,128]{1,0:T(8,128)S(1)}, u32[]{:S(2)}, u32[]{:S(2)}) collective-permute-start(f32[640,128]{1,0:T(8,128)S(1)} %get-tuple-element.25.refs_1_), channel_id=1, source_target_pairs={{0,4},{1,5},{2,6},{3,7},{4,0},{5,1},{6,2},{7,3},{8,12},{9,13},{10,... | collective-permute-start | bytes 983048 | tf_op jit(solution)/shard_map/ppermute | solution.py:48
  14.6 6.8 %collective-permute-start.4 = (f32[640,128]{1,0:T(8,128)S(1)}, f32[640,128]{1,0:T(8,128)S(1)}, u32[]{:S(2)}, u32[]{:S(2)}) collective-permute-start(f32[640,128]{1,0:T(8,128)S(1)} %get-tuple-element.27.refs_3_), channel_id=1, source_target_pairs={{32,64},{64,32},{96,128},{128,96},{160,192},{192,160},{224,256},{2... | collective-permute-start | bytes 983048 | tf_op jit(solution)/shard_map/ppermute | solution.py:40
  21.5 0.0 collective-permute-done.1.refs_0_
  21.5 0.0 copy-start
  21.5 0.8 %collective-permute-start.5 = (f32[640,128]{1,0:T(8,128)S(1)}, f32[640,128]{1,0:T(8,128)S(1)}, u32[]{:S(2)}, u32[]{:S(2)}) collective-permute-start(f32[640,128]{1,0:T(8,128)S(1)} %get-tuple-element.28.refs_4_), channel_id=1, source_target_pairs={{1,2},{5,6},{9,10},{13,14},{17,18},{21,22},{25,26},{29,30},{2,1},{... | collective-permute-start | bytes 983048 | tf_op jit(solution)/shard_map/ppermute | solution.py:48
  22.3 0.0 copy-start.1
  22.4 1.1 %copy-done = f32[1,6,384,384]{3,2,1,0:T(8,128)S(1)} copy-done((f32[1,6,384,384]{3,2,1,0:T(8,128)S(1)}, f32[1,6,384,384]{3,2,1,0:T(8,128)}, u32[]{:S(2)}) %copy-start) | copy-done | bytes 3538968
  23.5 1.6 %shard_map.79 = (bf16[6,128,384]{2,1,0:T(8,128)(2,1)S(1)}, bf16[6,128,384]{2,1,0:T(8,128)(2,1)S(1)}, f32[128,128]{1,0:T(8,128)S(1)}) custom-call(f32[1,6,384,384]{3,2,1,0:T(8,128)S(1)} %copy-done, f32[1536,128]{1,0:T(8,128)S(1)} %get-tuple-element.23.modes, f32[1,1536]{1,0:T(1,128)S(1)} %get-tuple-element.24.stiffness, f32[8,128]{1,0:T(8,128)S(1)} %shard_map.78.marker, ...), custom_call_target="tpu_custom_call" | custom-call | flops 800000000 | bytes 1000000 | tf_op jit(solution)/shard_map/pallas_call | solution.py:220
  25.1 0.0 collective-permute-done.refs_2_.partner
  25.1 0.0 collective-permute-done.2.refs_1_
  25.1 0.0 copy-done.1
  25.2 1.3 %shard_map.80 = (f32[3,128,128]{2,1,0:T(8,128)S(1)}, f32[128,256]{1,0:T(8,128)S(1)}, f32[128,256]{1,0:T(8,128)S(1)}) custom-call(s32[1,6]{1,0:T(1,128)S(1)} %copy-done.1, bf16[6,128,384]{2,1,0:T(8,128)(2,1)S(1)} %get-tuple-element.29.highs, bf16[6,128,384]{2,1,0:T(8,128)(2,1)S(1)} %get-tuple-element.30.lows, f32[128,128]{1,0:T(8,128)S(1)} %get-tuple-element.31.self_block, ...), custom_call_target="tpu_custom_call" | custom-call | flops 200000000 | bytes 1000000 | tf_op jit(solution)/shard_map/pallas_call | solution.py:220
  26.5 0.0 collective-permute-done.3.refs_0_
  26.5 2.8 %collective-permute-done.4.refs_1_ = f32[640,128]{1,0:T(8,128)S(1)} collective-permute-done((f32[640,128]{1,0:T(8,128)S(1)}, f32[640,128]{1,0:T(8,128)S(1)}, u32[]{:S(2)}, u32[]{:S(2)}) %collective-permute-start.4) | collective-permute-done | bytes 327712 | tf_op jit(solution)/shard_map/ppermute | solution.py:40
  29.3 0.0 collective-permute-done.5.refs_2_
  29.3 1.2 %shard_map.81 = (f32[3,128,128]{2,1,0:T(8,128)S(1)}, f32[128,768]{1,0:T(8,128)S(1)}) custom-call(s32[1,6]{1,0:T(1,128)S(1)} %copy-done.1, bf16[6,128,384]{2,1,0:T(8,128)(2,1)S(1)} %get-tuple-element.29.highs, bf16[6,128,384]{2,1,0:T(8,128)(2,1)S(1)} %get-tuple-element.30.lows, f32[128,256]{1,0:T(8,128)S(1)} %get-tuple-element.32.early_outer, ...), custom_call_target="tpu_custom_call" | custom-call | flops 200000000 | bytes 1000000 | tf_op jit(solution)/shard_map/pallas_call | solution.py:220
  30.5 2.7 %collective-permute-start.6 = (f32[128,768]{1,0:T(8,128)S(1)}, f32[128,768]{1,0:T(8,128)S(1)}, u32[]{:S(2)}, u32[]{:S(2)}) collective-permute-start(f32[128,768]{1,0:T(8,128)S(1)} %get-tuple-element.34.half), channel_id=1, source_target_pairs={{0,1},{1,0},{2,3},{3,2},{4,5},{5,4},{6,7},{7,6},{8,9},{9,8},{10,11... | collective-permute-start | bytes 1179656 | tf_op jit(solution)/shard_map/ppermute | solution.py:280
  33.3 1.1 %shard_map.82 = (bf16[2,128,128]{2,1,0:T(8,128)(2,1)S(1)}, f32[128,768]{1,0:T(8,128)S(1)}, f32[1,7,128,128]{3,2,1,0:T(8,128)}) custom-call(f32[640,128]{1,0:T(8,128)S(1)} %get-tuple-element.21.refs_0_.own, f32[640,128]{1,0:T(8,128)S(1)} %collective-permute-done.refs_2_.partner, f32[128,768]{1,0:T(8,128)S(1)} %get-tuple-element.34.half, ...), custom_call_target="tpu_custom_call" | custom-call | flops 150000000 | bytes 1000000 | tf_op jit(solution)/shard_map/pallas_call | solution.py:220
  34.4 0.2 collective-permute-done.6.partner_half
  34.6 0.3 shard_map.83
  34.9 16.3 %all_to_all.5.parts = f32[16,8,768]{2,1,0:T(8,128)S(1)} all-to-all(f32[16,8,768]{2,1,0:T(8,128)S(1)} %shard_map.83), channel_id=1, replica_groups={{0,2,4,6,8,10,12,14,16,18,20,22,24,26,28,30},{1,3,5,7,9,11,13,15,17,19,..., dimensions={0} | all-to-all | bytes 786432 | tf_op jit(solution)/shard_map/all_to_all | solution.py:304
  51.2 0.6 %shard_map.84 = f32[1,3,8,256]{3,2,1,0:T(8,128)} custom-call(f32[16,8,768]{2,1,0:T(8,128)S(1)} %all_to_all.5.parts), custom_call_target="tpu_custom_call" | custom-call | flops 1000000 | bytes 1000000 | tf_op jit(solution)/shard_map/pallas_call | solution.py:220
  (1 shorter events, 0.0 us)
Async XLA Ops:
  2.4 19.1 %collective-permute-start.1 = (f32[640,128]{1,0:T(8,128)S(1)}, f32[640,128]{1,0:T(8,128)S(1)}, u32[]{:S(2)}, u32[]{:S(2)}) collective-permute-start(f32[640,128]{1,0:T(8,128)S(1)} %get-tuple-element.21.refs_0_.own), channel_id=1, source_target_pairs={{4,8},{5,9},{6,10},{7,11},{8,4},{9,5},{10,6},{11,7},{12,16},{13,17... | collective-permute-start | bytes 983048 | tf_op jit(solution)/shard_map/ppermute | solution.py:48
  3.1 22.1 %collective-permute-start = (f32[640,128]{1,0:T(8,128)S(1)}, f32[640,128]{1,0:T(8,128)S(1)}, u32[]{:S(2)}, u32[]{:S(2)}) collective-permute-start(f32[640,128]{1,0:T(8,128)S(1)} %get-tuple-element.22.refs_5_), channel_id=1, source_target_pairs={{0,1},{4,5},{8,9},{12,13},{16,17},{20,21},{24,25},{28,29},{1,0},{5... | collective-permute-start | bytes 983048 | tf_op jit(solution)/shard_map/ppermute | solution.py:48
  5.0 20.1 %collective-permute-start.2 = (f32[640,128]{1,0:T(8,128)S(1)}, f32[640,128]{1,0:T(8,128)S(1)}, u32[]{:S(2)}, u32[]{:S(2)}) collective-permute-start(f32[640,128]{1,0:T(8,128)S(1)} %get-tuple-element.26.refs_2_), channel_id=1, source_target_pairs={{0,32},{32,0},{64,96},{96,64},{128,160},{160,128},{192,224},{224,1... | collective-permute-start | bytes 983048 | tf_op jit(solution)/shard_map/ppermute | solution.py:40
  7.0 19.4 %collective-permute-start.3 = (f32[640,128]{1,0:T(8,128)S(1)}, f32[640,128]{1,0:T(8,128)S(1)}, u32[]{:S(2)}, u32[]{:S(2)}) collective-permute-start(f32[640,128]{1,0:T(8,128)S(1)} %get-tuple-element.25.refs_1_), channel_id=1, source_target_pairs={{0,4},{1,5},{2,6},{3,7},{4,0},{5,1},{6,2},{7,3},{8,12},{9,13},{10,... | collective-permute-start | bytes 983048 | tf_op jit(solution)/shard_map/ppermute | solution.py:48
  14.6 14.7 %collective-permute-start.4 = (f32[640,128]{1,0:T(8,128)S(1)}, f32[640,128]{1,0:T(8,128)S(1)}, u32[]{:S(2)}, u32[]{:S(2)}) collective-permute-start(f32[640,128]{1,0:T(8,128)S(1)} %get-tuple-element.27.refs_3_), channel_id=1, source_target_pairs={{32,64},{64,32},{96,128},{128,96},{160,192},{192,160},{224,256},{2... | collective-permute-start | bytes 983048 | tf_op jit(solution)/shard_map/ppermute | solution.py:40
  21.5 2.0 %copy-start = (f32[1,6,384,384]{3,2,1,0:T(8,128)S(1)}, f32[1,6,384,384]{3,2,1,0:T(8,128)}, u32[]{:S(2)}) copy-start(f32[1,6,384,384]{3,2,1,0:T(8,128)} %couplings.1) | copy-start | bytes 10616836
  21.5 7.8 %collective-permute-start.5 = (f32[640,128]{1,0:T(8,128)S(1)}, f32[640,128]{1,0:T(8,128)S(1)}, u32[]{:S(2)}, u32[]{:S(2)}) collective-permute-start(f32[640,128]{1,0:T(8,128)S(1)} %get-tuple-element.28.refs_4_), channel_id=1, source_target_pairs={{1,2},{5,6},{9,10},{13,14},{17,18},{21,22},{25,26},{29,30},{2,1},{... | collective-permute-start | bytes 983048 | tf_op jit(solution)/shard_map/ppermute | solution.py:48
  22.3 2.8 %copy-start.1 = (s32[1,6]{1,0:T(1,128)S(1)}, s32[1,6]{1,0:T(1,128)}, u32[]{:S(2)}) copy-start(s32[1,6]{1,0:T(1,128)} %present.3) | copy-start | bytes 76
  30.5 4.1 %collective-permute-start.6 = (f32[128,768]{1,0:T(8,128)S(1)}, f32[128,768]{1,0:T(8,128)S(1)}, u32[]{:S(2)}, u32[]{:S(2)}) collective-permute-start(f32[128,768]{1,0:T(8,128)S(1)} %get-tuple-element.34.half), channel_id=1, source_target_pairs={{0,1},{1,0},{2,3},{3,2},{4,5},{5,4},{6,7},{7,6},{8,9},{9,8},{10,11... | collective-permute-start | bytes 1179656 | tf_op jit(solution)/shard_map/ppermute | solution.py:280

commit v3 on v2

--- a/solution.py
+++ b/solution.py
@@ -98,20 +98,21 @@
         pltpu.make_async_copy(modes, near_modes, sems.at[1]),
         pltpu.make_async_copy(stiffness, near_stiffness, sems.at[2]),
     ]
-    for out in outs:
-        for part in range(2):
-            source = basis.at[:, part * MODES : (part + 1) * MODES]
-            target = out.at[BLOCK + part * MODES : BLOCK + (part + 1) * MODES, :]
-            copies.append(pltpu.make_async_copy(source, target, sems.at[len(copies)]))
+    for part in range(2):
+        source = basis.at[:, part * MODES : (part + 1) * MODES]
+        target = outs[0].at[BLOCK + part * MODES : BLOCK + (part + 1) * MODES, :]
+        copies.append(pltpu.make_async_copy(source, target, sems.at[len(copies)]))
     for copy in copies:
         copy.start()
+    for copy in copies[2:]:
+        copy.wait()
+    for out in outs[1:]:
+        out[BLOCK:, :] = outs[0][BLOCK:, :]
     copies[0].wait()
     copies[1].wait()
     for direction, out in zip(slot_directions(), outs):
         first = pl.multiple_of(faces[0, direction] * BLOCK, BLOCK)
         out[:BLOCK, :] = near_modes[pl.ds(first, BLOCK), :]
-    for copy in copies[2:]:
-        copy.wait()
 
 
 def marker_kernel(marker):
@@ -236,7 +237,7 @@
         [pltpu.VMEM((PACKED, MODES), F32)] * DIRS
         + [pltpu.VMEM(mode_rows.shape, F32), pltpu.VMEM(stiffness.shape, F32)],
         [VMEM] * (DIRS + 2),
-        [pltpu.SMEM(own_face.shape, own_face.dtype), pltpu.SemaphoreType.DMA((3 + 2 * DIRS,))],
+        [pltpu.SMEM(own_face.shape, own_face.dtype), pltpu.SemaphoreType.DMA((5,))],
     )
     fetched = []
     for sent, (kind, odd) in zip(packed, EXCHANGES):

time: 52.1 us -> 51.7 us (level)
  no operation moved by 1% of the time
where the time goes in v3:
time: 51.7 us; the launch traced here: 51.4 us
  starting transfers between devices  22.6 us (44%)
  blocking collectives  16.3 us (32%)
  Pallas kernels  7.49 us (14%)
  waiting for transfers between devices  3.04 us (6%)
  local copies, waits for them, and re-layouts  1.16 us (2%)
  between operations  0.79 us (2%)
    all_to_all x1, blocking collectives, body(): parts = near(lax.all_to_all(terms, 'sub', 0, 0, axis_index_groups=chips))  16.3 us
    ppermute x4, starting transfers between devices, exchange(): return lax.ppermute(packed, 'sub', pairs)  11 us
    ppermute x2, starting transfers between devices, exchange(): return lax.ppermute(packed, 'group', swap_pairs(GROUPS, odd))  8.86 us
    pallas_call x8, Pallas kernels, call(): pl.pallas_call(kernel, out_shape=outs, in_specs=in_specs, out_specs=out_s...  7.49 us
    ppermute x2, waiting for transfers between devices, exchange(): return lax.ppermute(packed, 'group', swap_pairs(GROUPS, odd))  2.81 us
    ppermute x1, starting transfers between devices, body(): lax.ppermute(half, 'sub', [(i, i ^ 1) for i in range(SUBS)])  2.74 us
    unnamed x4, local copies, waits for them, and re-layouts  1.16 us
  transfers between devices with their start and end apart: 7, of which 2 were waited for; matrix products, arithmetic and copies ran while one was open for 0% of the time, Pallas kernels for 8%

profile of v3, /device:TPU:96, one launch (start us, length us, event | category | flops | bytes accessed | tf_op | source)
XLA Modules:
  0.0 51.4 jit_solution(11146600713631428339)
XLA Ops:
  0.6 1.3 %shard_map.77 = (f32[640,128]{1,0:T(8,128)S(1)}, f32[640,128]{1,0:T(8,128)S(1)}, f32[640,128]{1,0:T(8,128)S(1)}, f32[640,128]{1,0:T(8,128)S(1)}, f32[640,128]{1,...) custom-call(s32[1,6]{1,0:T(1,128)} %own_face.1, f32[1536,128]{1,0:T(8,128)} %modes.1, ...), custom_call_target="tpu_custom_call" | custom-call | flops 1000000 | bytes 1000000 | tf_op jit(solution)/shard_map/pallas_call | solution.py:221
  1.9 0.7 %collective-permute-start.1 = (f32[640,128]{1,0:T(8,128)S(1)}, f32[640,128]{1,0:T(8,128)S(1)}, u32[]{:S(2)}, u32[]{:S(2)}) collective-permute-start(f32[640,128]{1,0:T(8,128)S(1)} %get-tuple-element.21.refs_0_.own), channel_id=1, source_target_pairs={{4,8},{5,9},{6,10},{7,11},{8,4},{9,5},{10,6},{11,7},{12,16},{13,17... | collective-permute-start | bytes 983048 | tf_op jit(solution)/shard_map/ppermute | solution.py:48
  2.6 1.9 %collective-permute-start = (f32[640,128]{1,0:T(8,128)S(1)}, f32[640,128]{1,0:T(8,128)S(1)}, u32[]{:S(2)}, u32[]{:S(2)}) collective-permute-start(f32[640,128]{1,0:T(8,128)S(1)} %get-tuple-element.22.refs_5_), channel_id=1, source_target_pairs={{0,1},{4,5},{8,9},{12,13},{16,17},{20,21},{24,25},{28,29},{1,0},{5... | collective-permute-start | bytes 983048 | tf_op jit(solution)/shard_map/ppermute | solution.py:48
  4.6 2.0 %collective-permute-start.2 = (f32[640,128]{1,0:T(8,128)S(1)}, f32[640,128]{1,0:T(8,128)S(1)}, u32[]{:S(2)}, u32[]{:S(2)}) collective-permute-start(f32[640,128]{1,0:T(8,128)S(1)} %get-tuple-element.26.refs_2_), channel_id=1, source_target_pairs={{0,32},{32,0},{64,96},{96,64},{128,160},{160,128},{192,224},{224,1... | collective-permute-start | bytes 983048 | tf_op jit(solution)/shard_map/ppermute | solution.py:40
  6.6 7.6 %collective-permute-start.3 = (f32[640,128]{1,0:T(8,128)S(1)}, f32[640,128]{1,0:T(8,128)S(1)}, u32[]{:S(2)}, u32[]{:S(2)}) collective-permute-start(f32[640,128]{1,0:T(8,128)S(1)} %get-tuple-element.25.refs_1_), channel_id=1, source_target_pairs={{0,4},{1,5},{2,6},{3,7},{4,0},{5,1},{6,2},{7,3},{8,12},{9,13},{10,... | collective-permute-start | bytes 983048 | tf_op jit(solution)/shard_map/ppermute | solution.py:48
  14.2 6.8 %collective-permute-start.4 = (f32[640,128]{1,0:T(8,128)S(1)}, f32[640,128]{1,0:T(8,128)S(1)}, u32[]{:S(2)}, u32[]{:S(2)}) collective-permute-start(f32[640,128]{1,0:T(8,128)S(1)} %get-tuple-element.27.refs_3_), channel_id=1, source_target_pairs={{32,64},{64,32},{96,128},{128,96},{160,192},{192,160},{224,256},{2... | collective-permute-start | bytes 983048 | tf_op jit(solution)/shard_map/ppermute | solution.py:40
  21.0 0.0 collective-permute-done.1.refs_0_
  21.0 0.0 copy-start
  21.1 0.8 %collective-permute-start.5 = (f32[640,128]{1,0:T(8,128)S(1)}, f32[640,128]{1,0:T(8,128)S(1)}, u32[]{:S(2)}, u32[]{:S(2)}) collective-permute-start(f32[640,128]{1,0:T(8,128)S(1)} %get-tuple-element.28.refs_4_), channel_id=1, source_target_pairs={{1,2},{5,6},{9,10},{13,14},{17,18},{21,22},{25,26},{29,30},{2,1},{... | collective-permute-start | bytes 983048 | tf_op jit(solution)/shard_map/ppermute | solution.py:48
  21.9 0.0 copy-start.1
  21.9 1.1 %copy-done = f32[1,6,384,384]{3,2,1,0:T(8,128)S(1)} copy-done((f32[1,6,384,384]{3,2,1,0:T(8,128)S(1)}, f32[1,6,384,384]{3,2,1,0:T(8,128)}, u32[]{:S(2)}) %copy-start) | copy-done | bytes 3538968
  23.1 1.6 %shard_map.79 = (bf16[6,128,384]{2,1,0:T(8,128)(2,1)S(1)}, bf16[6,128,384]{2,1,0:T(8,128)(2,1)S(1)}, f32[128,128]{1,0:T(8,128)S(1)}) custom-call(f32[1,6,384,384]{3,2,1,0:T(8,128)S(1)} %copy-done, f32[1536,128]{1,0:T(8,128)S(1)} %get-tuple-element.23.modes, f32[1,1536]{1,0:T(1,128)S(1)} %get-tuple-element.24.stiffness, f32[8,128]{1,0:T(8,128)S(1)} %shard_map.78.marker, ...), custom_call_target="tpu_custom_call" | custom-call | flops 800000000 | bytes 1000000 | tf_op jit(solution)/shard_map/pallas_call | solution.py:221
  24.7 0.0 collective-permute-done.refs_2_.partner
  24.7 0.0 collective-permute-done.2.refs_1_
  24.7 0.0 copy-done.1
  24.7 1.3 %shard_map.80 = (f32[3,128,128]{2,1,0:T(8,128)S(1)}, f32[128,256]{1,0:T(8,128)S(1)}, f32[128,256]{1,0:T(8,128)S(1)}) custom-call(s32[1,6]{1,0:T(1,128)S(1)} %copy-done.1, bf16[6,128,384]{2,1,0:T(8,128)(2,1)S(1)} %get-tuple-element.29.highs, bf16[6,128,384]{2,1,0:T(8,128)(2,1)S(1)} %get-tuple-element.30.lows, f32[128,128]{1,0:T(8,128)S(1)} %get-tuple-element.31.self_block, ...), custom_call_target="tpu_custom_call" | custom-call | flops 200000000 | bytes 1000000 | tf_op jit(solution)/shard_map/pallas_call | solution.py:221
  26.0 0.0 collective-permute-done.3.refs_0_
  26.0 2.8 %collective-permute-done.4.refs_1_ = f32[640,128]{1,0:T(8,128)S(1)} collective-permute-done((f32[640,128]{1,0:T(8,128)S(1)}, f32[640,128]{1,0:T(8,128)S(1)}, u32[]{:S(2)}, u32[]{:S(2)}) %collective-permute-start.4) | collective-permute-done | bytes 327712 | tf_op jit(solution)/shard_map/ppermute | solution.py:40
  28.8 0.0 collective-permute-done.5.refs_2_
  28.8 1.2 %shard_map.81 = (f32[3,128,128]{2,1,0:T(8,128)S(1)}, f32[128,768]{1,0:T(8,128)S(1)}) custom-call(s32[1,6]{1,0:T(1,128)S(1)} %copy-done.1, bf16[6,128,384]{2,1,0:T(8,128)(2,1)S(1)} %get-tuple-element.29.highs, bf16[6,128,384]{2,1,0:T(8,128)(2,1)S(1)} %get-tuple-element.30.lows, f32[128,256]{1,0:T(8,128)S(1)} %get-tuple-element.32.early_outer, ...), custom_call_target="tpu_custom_call" | custom-call | flops 200000000 | bytes 1000000 | tf_op jit(solution)/shard_map/pallas_call | solution.py:221
  30.1 2.7 %collective-permute-start.6 = (f32[128,768]{1,0:T(8,128)S(1)}, f32[128,768]{1,0:T(8,128)S(1)}, u32[]{:S(2)}, u32[]{:S(2)}) collective-permute-start(f32[128,768]{1,0:T(8,128)S(1)} %get-tuple-element.34.half), channel_id=1, source_target_pairs={{0,1},{1,0},{2,3},{3,2},{4,5},{5,4},{6,7},{7,6},{8,9},{9,8},{10,11... | collective-permute-start | bytes 1179656 | tf_op jit(solution)/shard_map/ppermute | solution.py:281
  32.8 1.1 %shard_map.82 = (bf16[2,128,128]{2,1,0:T(8,128)(2,1)S(1)}, f32[128,768]{1,0:T(8,128)S(1)}, f32[1,7,128,128]{3,2,1,0:T(8,128)}) custom-call(f32[640,128]{1,0:T(8,128)S(1)} %get-tuple-element.21.refs_0_.own, f32[640,128]{1,0:T(8,128)S(1)} %collective-permute-done.refs_2_.partner, f32[128,768]{1,0:T(8,128)S(1)} %get-tuple-element.34.half, ...), custom_call_target="tpu_custom_call" | custom-call | flops 150000000 | bytes 1000000 | tf_op jit(solution)/shard_map/pallas_call | solution.py:221
  33.9 0.2 collective-permute-done.6.partner_half
  34.1 0.3 shard_map.83
  34.5 16.3 %all_to_all.5.parts = f32[16,8,768]{2,1,0:T(8,128)S(1)} all-to-all(f32[16,8,768]{2,1,0:T(8,128)S(1)} %shard_map.83), channel_id=1, replica_groups={{0,2,4,6,8,10,12,14,16,18,20,22,24,26,28,30},{1,3,5,7,9,11,13,15,17,19,..., dimensions={0} | all-to-all | bytes 786432 | tf_op jit(solution)/shard_map/all_to_all | solution.py:305
  50.7 0.6 %shard_map.84 = f32[1,3,8,256]{3,2,1,0:T(8,128)} custom-call(f32[16,8,768]{2,1,0:T(8,128)S(1)} %all_to_all.5.parts), custom_call_target="tpu_custom_call" | custom-call | flops 1000000 | bytes 1000000 | tf_op jit(solution)/shard_map/pallas_call | solution.py:221
  (1 shorter events, 0.0 us)
Async XLA Ops:
  1.9 19.1 %collective-permute-start.1 = (f32[640,128]{1,0:T(8,128)S(1)}, f32[640,128]{1,0:T(8,128)S(1)}, u32[]{:S(2)}, u32[]{:S(2)}) collective-permute-start(f32[640,128]{1,0:T(8,128)S(1)} %get-tuple-element.21.refs_0_.own), channel_id=1, source_target_pairs={{4,8},{5,9},{6,10},{7,11},{8,4},{9,5},{10,6},{11,7},{12,16},{13,17... | collective-permute-start | bytes 983048 | tf_op jit(solution)/shard_map/ppermute | solution.py:48
  2.6 22.0 %collective-permute-start = (f32[640,128]{1,0:T(8,128)S(1)}, f32[640,128]{1,0:T(8,128)S(1)}, u32[]{:S(2)}, u32[]{:S(2)}) collective-permute-start(f32[640,128]{1,0:T(8,128)S(1)} %get-tuple-element.22.refs_5_), channel_id=1, source_target_pairs={{0,1},{4,5},{8,9},{12,13},{16,17},{20,21},{24,25},{28,29},{1,0},{5... | collective-permute-start | bytes 983048 | tf_op jit(solution)/shard_map/ppermute | solution.py:48
  4.6 20.1 %collective-permute-start.2 = (f32[640,128]{1,0:T(8,128)S(1)}, f32[640,128]{1,0:T(8,128)S(1)}, u32[]{:S(2)}, u32[]{:S(2)}) collective-permute-start(f32[640,128]{1,0:T(8,128)S(1)} %get-tuple-element.26.refs_2_), channel_id=1, source_target_pairs={{0,32},{32,0},{64,96},{96,64},{128,160},{160,128},{192,224},{224,1... | collective-permute-start | bytes 983048 | tf_op jit(solution)/shard_map/ppermute | solution.py:40
  6.6 19.4 %collective-permute-start.3 = (f32[640,128]{1,0:T(8,128)S(1)}, f32[640,128]{1,0:T(8,128)S(1)}, u32[]{:S(2)}, u32[]{:S(2)}) collective-permute-start(f32[640,128]{1,0:T(8,128)S(1)} %get-tuple-element.25.refs_1_), channel_id=1, source_target_pairs={{0,4},{1,5},{2,6},{3,7},{4,0},{5,1},{6,2},{7,3},{8,12},{9,13},{10,... | collective-permute-start | bytes 983048 | tf_op jit(solution)/shard_map/ppermute | solution.py:48
  14.2 14.7 %collective-permute-start.4 = (f32[640,128]{1,0:T(8,128)S(1)}, f32[640,128]{1,0:T(8,128)S(1)}, u32[]{:S(2)}, u32[]{:S(2)}) collective-permute-start(f32[640,128]{1,0:T(8,128)S(1)} %get-tuple-element.27.refs_3_), channel_id=1, source_target_pairs={{32,64},{64,32},{96,128},{128,96},{160,192},{192,160},{224,256},{2... | collective-permute-start | bytes 983048 | tf_op jit(solution)/shard_map/ppermute | solution.py:40
  21.0 2.0 %copy-start = (f32[1,6,384,384]{3,2,1,0:T(8,128)S(1)}, f32[1,6,384,384]{3,2,1,0:T(8,128)}, u32[]{:S(2)}) copy-start(f32[1,6,384,384]{3,2,1,0:T(8,128)} %couplings.1) | copy-start | bytes 10616836
  21.1 7.8 %collective-permute-start.5 = (f32[640,128]{1,0:T(8,128)S(1)}, f32[640,128]{1,0:T(8,128)S(1)}, u32[]{:S(2)}, u32[]{:S(2)}) collective-permute-start(f32[640,128]{1,0:T(8,128)S(1)} %get-tuple-element.28.refs_4_), channel_id=1, source_target_pairs={{1,2},{5,6},{9,10},{13,14},{17,18},{21,22},{25,26},{29,30},{2,1},{... | collective-permute-start | bytes 983048 | tf_op jit(solution)/shard_map/ppermute | solution.py:48
  21.9 2.8 %copy-start.1 = (s32[1,6]{1,0:T(1,128)S(1)}, s32[1,6]{1,0:T(1,128)}, u32[]{:S(2)}) copy-start(s32[1,6]{1,0:T(1,128)} %present.3) | copy-start | bytes 76
  30.1 4.1 %collective-permute-start.6 = (f32[128,768]{1,0:T(8,128)S(1)}, f32[128,768]{1,0:T(8,128)S(1)}, u32[]{:S(2)}, u32[]{:S(2)}) collective-permute-start(f32[128,768]{1,0:T(8,128)S(1)} %get-tuple-element.34.half), channel_id=1, source_target_pairs={{0,1},{1,0},{2,3},{3,2},{4,5},{5,4},{6,7},{7,6},{8,9},{9,8},{10,11... | collective-permute-start | bytes 1179656 | tf_op jit(solution)/shard_map/ppermute | solution.py:281
